TPU v7x, 128 devices: a whole 4x4x4 slice. The times are simulated.
128 devices in a mesh: region: 8 (over y, core), slab: 16 (over x, z).
Axes of the slice: x: 4, y: 4, z: 4, core: 2. Of those that a mesh axis runs over, the one named last changes fastest.
Arguments:
- coarse: float32 [32, 176, 8, 256], P('region', 'slab'), may hold values from -6 to 6
- cover: int32 [8, 16, 16, 3], replicated, may hold values from 0 to 175, as said below
- sizes: int32 [8, 2], replicated, may hold values from 6 to 16, as said below
- tclass: int32 [8, 48, 192], P('region'), may hold values from 0 to 15
- up_rows: float32 [384, 128], replicated, may hold values from -0.5 to 0.5
- up_cols: float32 [128, 1536], replicated, may hold values from -0.5 to 0.5
- lift: float32 [32, 64], replicated, may hold values from -1 to 1
- kernel_one: bfloat16 [3, 3, 64, 64], replicated, may hold values from -0.25 to 0.25
- kernel_two: bfloat16 [3, 3, 64, 64], replicated, may hold values from -0.25 to 0.25
- gain_table: float32 [16, 64], replicated, may hold values from 0.1 to 1.9
- shift_table: float32 [16, 64], replicated, may hold values from -3 to 3
Outputs:
- fine_out: bfloat16 [8, 384, 98304], P('region', 'slab')
Inputs may be any that keep to these rules, and one draw needn't show every extreme that they name: `cover`: for each region r there is an anchor (g, h) such that entry (r, i, j) names global block row g + i and block column (h + j) % 176 (longitude wraps around), as owner (g + i) // 4, row (g + i) % 4 and that column. `sizes`: column 0 lies in 6 to 16, column 1 in 6 to 16; in every draw one region has both full and another has both least.
All inputs are finite; a program needn't handle non-finite values.
Results may differ from a plain program's by a relative error of at most 0.0053.
Values may be sent and summed in bfloat16 or wider, within the bound.
A program may use at most 192 MiB of HBM per device.

v0:
```python
import jax
import jax.numpy as jnp
from jax import lax
from jax.sharding import PartitionSpec as P


def extended(cells, sides, width):
    for axis, dim in sides:
        count = lax.axis_size(axis)
        ends = count - 1
        head = lax.slice_in_dim(cells, 0, width, axis=dim)
        tail = lax.slice_in_dim(cells, cells.shape[dim] - width, cells.shape[dim], axis=dim)
        cells = jnp.concatenate(
            [
                lax.ppermute(tail, axis, [(i, (i + 1) % count) for i in range(ends)]),
                cells,
                lax.ppermute(head, axis, [((i + 1) % count, i) for i in range(ends)]),
            ],
            axis=dim,
        )
    return cells


def pair_kernel(kernel):
    channels = kernel.shape[2]
    empty_block = jnp.zeros((3, channels, channels), kernel.dtype)
    groups = []
    for offset in (-1, 0, 1):
        rows_in = []
        for side_in in (0, 1):
            cols_out = []
            for side_out in (0, 1):
                column = 2 * offset + side_in - side_out + 1
                if 0 <= column <= 2:
                    cols_out.append(kernel[:, column])
                else:
                    cols_out.append(empty_block)
            rows_in.append(jnp.concatenate(cols_out, axis=2))
        groups.append(jnp.concatenate(rows_in, axis=1))
    return jnp.concatenate(groups, axis=1)


def conv_pairs(padded, weights, out_rows):
    pair_count = padded.shape[1]
    zero_edge = jnp.zeros((padded.shape[0], 1, padded.shape[2]), padded.dtype)
    widened = jnp.concatenate([zero_edge, padded, zero_edge], axis=1)
    stacked = jnp.concatenate(
        [widened[:, 0:pair_count], widened[:, 1 : pair_count + 1], widened[:, 2 : pair_count + 2]],
        axis=2,
    )
    summed = None
    for shift_row in range(3):
        partial_value = jnp.einsum(
            "ypk,kn->ypn",
            stacked[shift_row : shift_row + out_rows],
            weights[shift_row],
            preferred_element_type=jnp.float32,
        )
        summed = partial_value if summed is None else summed + partial_value
    return summed


def local(
    coarse,
    cover,
    sizes,
    tclass,
    up_rows,
    up_cols,
    lift,
    kernel_one,
    kernel_two,
    gain_table,
    shift_table,
):
    band = lax.all_gather(coarse, "slab", axis=1, tiled=True)
    n_slab = lax.axis_size("slab")
    owner = lax.axis_index("region")
    slab_index = lax.axis_index("slab")
    block_rows = cover.shape[1]
    block_cols = cover.shape[2]
    block_height = band.shape[2]
    block_span = band.shape[3]
    in_channels = lift.shape[0]
    channels = lift.shape[1]
    fine_rows = up_rows.shape[0]
    fine_cols = up_cols.shape[1]
    rows_dev = fine_rows // n_slab
    pair_count = fine_cols // 2
    col_share = block_cols // n_slab
    rows_full = up_rows.reshape(fine_rows, block_rows, block_height)
    covered = cover
    covered = lax.dynamic_slice_in_dim(covered, slab_index * col_share, col_share, 2)
    blocks = band[covered[..., 1], covered[..., 2]]
    mine = covered[..., 0] == owner
    blocks = jnp.where(mine[..., None, None], blocks, 0.0)
    partial_cols = lax.psum_scatter(
        jnp.einsum(
            "ykb,rkjbw->ryjw",
            rows_full,
            blocks,
            precision=lax.Precision.HIGHEST,
            preferred_element_type=jnp.float32,
        ),
        "region",
        scatter_dimension=0,
        tiled=True,
    )
    partial_rows = lax.all_to_all(partial_cols, "slab", split_axis=1, concat_axis=2, tiled=True)
    partial_rows = partial_rows[0].reshape(
        rows_dev, block_cols, block_span // in_channels, in_channels
    )
    cols_op = up_cols.reshape(block_cols, block_span // in_channels, fine_cols)
    upsampled = jnp.einsum("ykwc,kwx->ycx", partial_rows, cols_op, precision=lax.Precision.HIGHEST)
    lifted = jnp.einsum("ycx,cd->yxd", upsampled, lift, precision=lax.Precision.HIGHEST)
    lifted = lifted.reshape(rows_dev, pair_count, 2 * channels)
    region_size = sizes[owner]
    valid_rows = region_size[0] * (fine_rows // block_rows)
    valid_cols = region_size[1] * (fine_cols // block_cols)
    col_index = (
        2 * jnp.arange(pair_count, dtype=jnp.int32)[:, None]
        + jnp.arange(2 * channels, dtype=jnp.int32)[None, :] // channels
    )
    col_valid = col_index < valid_cols

    def row_valid(first_row, row_count):
        global_rows = first_row + jnp.arange(row_count, dtype=jnp.int32)
        return (global_rows, (global_rows >= 0) & (global_rows < valid_rows))

    own_rows, own_valid = row_valid(slab_index * rows_dev, rows_dev)
    inside = own_valid[:, None, None] & col_valid[None]
    fine_in = jnp.where(inside, lifted, 0.0).astype(jnp.bfloat16)
    activated = jax.nn.silu(fine_in.astype(jnp.float32)).astype(jnp.bfloat16)
    tile_count = tclass.shape[1]
    tile_cols = tclass.shape[2]
    tile_rows = fine_rows // tile_count
    class_ids = jnp.arange(gain_table.shape[0], dtype=jnp.int32)
    weights_one = pair_kernel(kernel_one)
    weights_two = pair_kernel(kernel_two)
    padded = extended(activated, (("slab", 0),), 1)
    first_conv = conv_pairs(padded, weights_one, rows_dev)
    row_count = first_conv.shape[0]
    global_rows, valid = row_valid(slab_index * rows_dev, row_count)
    tile_index = jnp.clip(global_rows // tile_rows, 0, tile_count - 1)
    row_classes = tclass[0][tile_index]
    onehot = (row_classes[..., None] == class_ids[None, None, :]).astype(jnp.float32)
    gain_rows = jnp.einsum("rtk,kc->rtc", onehot, gain_table, precision=lax.Precision.HIGHEST)
    shift_rows = jnp.einsum("rtk,kc->rtc", onehot, shift_table, precision=lax.Precision.HIGHEST)
    gain_rows = jnp.concatenate([gain_rows, gain_rows], axis=-1)
    shift_rows = jnp.concatenate([shift_rows, shift_rows], axis=-1)
    shaped = first_conv.reshape(row_count, tile_cols, pair_count // tile_cols, 2 * channels)
    modulated = shaped * gain_rows[:, :, None, :] + shift_rows[:, :, None, :]
    modulated = modulated.reshape(row_count, pair_count, 2 * channels)
    retain = valid[:, None, None] & col_valid[None]
    hidden = jnp.where(retain, jax.nn.silu(modulated), 0.0).astype(jnp.bfloat16)
    padded_hidden = extended(hidden, (("slab", 0),), 1)
    second_conv = conv_pairs(padded_hidden, weights_two, rows_dev)
    result = jnp.where(inside, fine_in.astype(jnp.float32) + second_conv, 0.0).astype(jnp.bfloat16)
    return result.reshape(1, rows_dev, pair_count * 2 * channels)


def solution(mesh):
    return jax.shard_map(
        local,
        mesh=mesh,
        in_specs=(
            P("region", "slab", None, None),
            P(),
            P(),
            P("region", None, None),
            P(),
            P(),
            P(),
            P(),
            P(),
            P(),
            P(),
        ),
        out_specs=P("region", "slab", None),
        check_vma=False,
    )
```

profile of v0, /device:TPU:96, one launch (start us, length us, event | category | flops | bytes accessed | tf_op | source)
XLA Modules:
  0.0 313.4 jit_solution(15487417491095555489)
XLA Ops:
  6.6 0.7 all-gather.2.cloned.1.call-update
  7.3 1.0 constant_dynamic-slice_fusion.1
  8.8 1.1 copy.39
  9.9 59.4 %all-gather.2.cloned.1.call-done = f32[4,176,8,256]{3,2,1,0:T(8,128)} async-done(((f32[4,11,8,256]{3,2,1,0:T(8,128)}), f32[4,176,8,256]{3,2,1,0:T(8,128)}) %all-gather.2.cloned.1.call-update) | async-done | bytes 5767184 | tf_op jit(solution)/shard_map/all_gather | solution.py:76
  69.3 3.5 %gather_fusion = f32[128,8,256]{2,1,0:T(8,128)S(1)} fusion(f32[4,176,8,256]{3,2,1,0:T(8,128)} %all-gather.2.cloned.1.call-done, s32[128]{0:T(128)S(1)} %reshape.210), kind=kCustom, calls=%fused_computation | custom fusion | bytes 2098176 | tf_op jit(solution)/shard_map/gather | solution.py:94
  72.8 4.6 %convolution_bitcast_fusion = f32[8,384,1,256]{1,3,0,2:T(8,128)} fusion(f32[8,16,8,256]{3,2,1,0:T(8,128)S(1)} %bitcast.104, pred[8,16]{1,0:T(8,128)(4,1)S(1)} %compare_bitcast_fusion, f32[384,16,8]{0,2,1:T(8,128)S(1)} %bitcast.106), kind=kOutput, calls=%fused_computation.27 | convolution fusion | flops 1208221696 | bytes 4391040 | tf_op jit(solution)/shard_map/ykb,rkjbw->ryjw/dot_general | solution.py:98
  78.8 0.6 gather_fusion.1
  79.4 0.6 constant_dynamic-update-slice_fusion.3
  80.4 0.8 fusion.14
  81.3 2.1 pad_maximum_fusion.4
  83.3 0.8 fusion.13
  84.1 2.0 pad_maximum_fusion.5
  86.2 0.7 slice_bitcast_fusion.12
  86.8 26.5 %reduce-scatter.2.cloned.1.call-done = f32[1,384,1,256]{1,3,0,2:T(8,128)} async-done(((f32[8,384,1,256]{1,3,0,2:T(8,128)}), f32[1,384,1,256]{1,3,0,2:T(8,128)}) %reduce-scatter.2.cloned.1.call-update) | async-done | bytes 393232 | tf_op jit(solution)/shard_map/reduce_scatter | solution.py:97
  113.4 1.9 copy.41
  115.2 7.1 %all-to-all-start = ((f32[1,384,1,256]{3,0,2,1:T(1,128)}), f32[1,384,1,256]{3,0,2,1:T(1,128)S(1)}, u32[]{:S(2)}, u32[]{:S(2)}) async-start(f32[1,384,1,256]{3,0,2,1:T(1,128)} %copy.41), calls=%async_computation.1 | async-start | bytes 786432 | tf_op jit(solution)/shard_map/all_to_all | solution.py:109
  122.9 2.4 copy.46
  125.3 3.4 %copy.47 = f32[24,192,128]{2,1,0:T(8,128)} copy(f32[24,192,128]{1,2,0:T(8,128)} %pad_maximum_fusion.5) | data formatting | bytes 4718592 | tf_op jit(solution)/shard_map/concatenate | solution.py:150
  129.4 1.4 pad_dynamic-update-slice_fusion.1
  130.8 0.8 add_compare_fusion
  131.6 0.8 copy.54
  132.4 2.5 reshape_squeeze.3
  134.9 5.7 %fusion.9 = f32[24,32,1536,1]{2,1,0,3:T(8,128)S(1)} fusion(f32[24,16,8,32]{3,2,0,1:T(8,128)} %reshape_squeeze.3, f32[128,1536]{1,0:T(8,128)S(1)} %copy-done), kind=kOutput, calls=%fused_computation.29 | convolution fusion | flops 1811939328 | bytes 5898240 | tf_op jit(solution)/shard_map/ykwc,kwx->ycx/dot_general | solution.py:114
  140.6 31.9 %fusion.7 = bf16[24,1536,64]{2,1,0:T(8,128)(2,1)} fusion(f32[24,32,1536,1]{2,1,0,3:T(8,128)S(1)} %fusion.9, f32[32,64]{1,0:T(8,128)S(1)} %copy-done.14), kind=kOutput, calls=%fused_computation.23 | convolution fusion | flops 905969664 | bytes 9445376 | tf_op jit(solution)/shard_map/ycx,cd->yxd/dot_general | solution.py:115
  172.5 12.7 %reshape.206 = bf16[24,768,128]{2,1,0:T(8,128)(2,1)} reshape(bf16[24,1536,64]{2,1,0:T(8,128)(2,1)} %fusion.7) | data formatting | bytes 9437184 | tf_op jit(solution)/shard_map/reshape | solution.py:116
  185.2 4.9 %fusion.3 = bf16[24,768,128]{2,1,0:T(8,128)(2,1)S(1)} fusion(bf16[24,768,128]{2,1,0:T(8,128)(2,1)} %reshape.206, pred[768,128]{1,0:T(8,128)(4,1)S(1)} %copy-done.11, pred[24]{0:T(512)(128)(4,1)S(1)} %copy-done.21), kind=kLoop, calls=%fused_computation.13 | loop fusion | flops 18874368 | bytes 9535512 | tf_op jit(solution)/shard_map/convert_element_type | solution.py:133
  190.2 3.4 %collective-permute-start = (bf16[1,768,128]{2,1,0:T(8,128)(2,1)S(1)}, bf16[1,768,128]{2,1,0:T(8,128)(2,1)S(1)}, u32[]{:S(2)}, u32[]{:S(2)}) collective-permute-start(bf16[1,768,128]{2,1,0:T(8,128)(2,1)S(1)} %get-tuple-element.11), channel_id=1, source_target_pairs={{0,1},{1,2},{2,3},{3,4},{4,5},{5,6},{6,7},{7,8},{8,9},{9,10},{10,1... | collective-permute-start | bytes 589832 | tf_op jit(solution)/shard_map/ppermute | solution.py:15
  193.6 2.5 collective-permute-start.1
  196.1 0.7 maximum_dynamic-update-slice_fusion.3
  196.8 0.7 maximum_dynamic-update-slice_fusion.2
  197.7 5.5 %collective-permute-done.1 = bf16[1,768,128]{2,1,0:T(8,128)(2,1)S(1)} collective-permute-done((bf16[1,768,128]{2,1,0:T(8,128)(2,1)S(1)}, bf16[1,768,128]{2,1,0:T(8,128)(2,1)S(1)}, u32[]{:S(2)}, u32[]{:S(2)}) %collective-permute-start.1) | collective-permute-done | bytes 196640 | tf_op jit(solution)/shard_map/ppermute | solution.py:17
  203.2 0.7 pad_maximum_fusion.2
  203.9 4.0 %pad_slice_fusion.3 = (bf16[26,768,128]{2,1,0:T(8,128)(2,1)S(1)}, bf16[26,768,128]{2,1,0:T(8,128)(2,1)S(1)}) fusion(bf16[26,768,128]{2,1,0:T(8,128)(2,1)S(1)} %pad_maximum_fusion.2), kind=kLoop, calls=%fused_computation.20 | loop fusion | bytes 15335424 | tf_op jit(solution)/shard_map/slice | solution.py:48
  208.0 8.5 %fusion.21 = f32[24,768,128]{2,1,0:T(8,128)} fusion(bf16[3,384,128]{2,1,0:T(8,128)(2,1)S(1)} %copy-done.19, bf16[26,768,128]{2,1,0:T(8,128)(2,1)S(1)} %get-tuple-element.8, bf16[1,768,128]{2,1,0:T(8,128)(2,1)S(1)} %collective-permute-done.1, bf16[24,768,128]{2,1,0:T(8,128)(2,1)S(1)} %fusion.3, bf16[1,768,128]{2,1,0:T(8,128)(2,1)S(1)} %collective-permute-done, ...), kind=kOutput, calls=%fused_computation.48 | convolution fusion | flops 1888616448 | bytes 24870912 | tf_op jit(solution)/shard_map/ypk,kn->ypn/dot_general | solution.py:53
  216.5 7.4 %fusion.22 = f32[24,768,128]{2,1,0:T(8,128)} fusion(bf16[3,384,128]{2,1,0:T(8,128)(2,1)S(1)} %copy-done.19, bf16[26,768,128]{2,1,0:T(8,128)(2,1)S(1)} %get-tuple-element.8, bf16[1,768,128]{2,1,0:T(8,128)(2,1)S(1)} %collective-permute-done.1, bf16[24,768,128]{2,1,0:T(8,128)(2,1)S(1)} %fusion.3, bf16[1,768,128]{2,1,0:T(8,128)(2,1)S(1)} %collective-permute-done, ...), kind=kOutput, calls=%fused_computation.50 | convolution fusion | flops 1888616448 | bytes 24870912 | tf_op jit(solution)/shard_map/ypk,kn->ypn/dot_general | solution.py:53
  223.9 5.3 %mul.53 = f32[24,192,4,128]{3,2,1,0:T(4,128)} broadcast(f32[24,192,128]{2,1,0:T(8,128)S(1)} %copy.46), dimensions={0,1,3} | broadcast | bytes 11796480 | tf_op jit(solution)/shard_map/mul | solution.py:152
  229.2 7.0 %add.156 = f32[24,192,4,128]{3,2,1,0:T(4,128)} broadcast(f32[24,192,128]{2,1,0:T(8,128)} %copy.47), dimensions={0,1,3} | broadcast | bytes 11796480 | tf_op jit(solution)/shard_map/add | solution.py:152
  236.2 18.3 %fusion.5 = bf16[24,768,128]{2,1,0:T(8,128)(2,1)S(1)} fusion(f32[24,768,128]{2,1,0:T(8,128)} %bitcast.102, f32[24,768,128]{2,1,0:T(8,128)} %bitcast.101, f32[24,768,128]{2,1,0:T(8,128)} %fusion.22, f32[24,768,128]{2,1,0:T(8,128)} %fusion.21, pred[768,128]{1,0:T(8,128)(4,1)S(1)} %copy-done.11, pred[24]{0:T(512)(128)(4,1)S(1)} %copy-done.21, ...), kind=kOutput, calls=%fused_computation.15 | convolution fusion | flops 1914568704 | bytes 57999872 | tf_op jit(solution)/shard_map/ypk,kn->ypn/dot_general | solution.py:53
  254.5 1.9 collective-permute-start.2
  256.5 3.9 %collective-permute-start.3 = (bf16[1,768,128]{2,1,0:T(8,128)(2,1)S(1)}, bf16[1,768,128]{2,1,0:T(8,128)(2,1)S(1)}, u32[]{:S(2)}, u32[]{:S(2)}) collective-permute-start(bf16[1,768,128]{2,1,0:T(8,128)(2,1)S(1)} %get-tuple-element.10), channel_id=1, source_target_pairs={{1,0},{2,1},{3,2},{4,3},{5,4},{6,5},{7,6},{8,7},{9,8},{10,9},{11,1... | collective-permute-start | bytes 589832 | tf_op jit(solution)/shard_map/ppermute | solution.py:17
  260.5 1.6 collective-permute-done.2
  262.1 4.0 %collective-permute-done.3 = bf16[1,768,128]{2,1,0:T(8,128)(2,1)S(1)} collective-permute-done((bf16[1,768,128]{2,1,0:T(8,128)(2,1)S(1)}, bf16[1,768,128]{2,1,0:T(8,128)(2,1)S(1)}, u32[]{:S(2)}, u32[]{:S(2)}) %collective-permute-start.3) | collective-permute-done | bytes 196640 | tf_op jit(solution)/shard_map/ppermute | solution.py:17
  266.1 0.7 pad_maximum_fusion.3
  266.8 4.0 %pad_slice_fusion.1 = (bf16[26,768,128]{2,1,0:T(8,128)(2,1)S(1)}, bf16[26,768,128]{2,1,0:T(8,128)(2,1)S(1)}) fusion(bf16[26,768,128]{2,1,0:T(8,128)(2,1)S(1)} %pad_maximum_fusion.3), kind=kLoop, calls=%fused_computation.18 | loop fusion | bytes 15335424 | tf_op jit(solution)/shard_map/slice | solution.py:48
  270.9 8.0 %fusion.19 = f32[24,768,128]{2,1,0:T(8,128)} fusion(bf16[3,384,128]{2,1,0:T(8,128)(2,1)S(1)} %constant_dynamic-update-slice_fusion.2, bf16[26,768,128]{2,1,0:T(8,128)(2,1)S(1)} %get-tuple-element.6, bf16[1,768,128]{2,1,0:T(8,128)(2,1)S(1)} %collective-permute-done.3, bf16[24,768,128]{2,1,0:T(8,128)(2,1)S(1)} %fusion.5, ...), kind=kOutput, calls=%fused_computation.43 | convolution fusion | flops 1888616448 | bytes 24870912 | tf_op jit(solution)/shard_map/ypk,kn->ypn/dot_general | solution.py:53
  278.9 7.4 %fusion.20 = f32[24,768,128]{2,1,0:T(8,128)} fusion(bf16[3,384,128]{2,1,0:T(8,128)(2,1)S(1)} %constant_dynamic-update-slice_fusion.2, bf16[26,768,128]{2,1,0:T(8,128)(2,1)S(1)} %get-tuple-element.6, bf16[1,768,128]{2,1,0:T(8,128)(2,1)S(1)} %collective-permute-done.3, bf16[24,768,128]{2,1,0:T(8,128)(2,1)S(1)} %fusion.5, ...), kind=kOutput, calls=%fused_computation.45 | convolution fusion | flops 1888616448 | bytes 24870912 | tf_op jit(solution)/shard_map/ypk,kn->ypn/dot_general | solution.py:53
  286.3 13.8 %fusion.6 = bf16[24,768,128]{2,1,0:T(8,128)(2,1)} fusion(f32[24,768,128]{2,1,0:T(8,128)} %fusion.20, f32[24,768,128]{2,1,0:T(8,128)} %fusion.19, pred[768,128]{1,0:T(8,128)(4,1)S(1)} %copy-done.11, pred[24]{0:T(512)(128)(4,1)S(1)} %copy-done.21, bf16[3,384,128]{2,1,0:T(8,128)(2,1)S(1)} %constant_dynamic-update-slice_fusion.2, ...), kind=kOutput, calls=%fused_computation.16 | convolution fusion | flops 1907490816 | bytes 43844096 | tf_op jit(solution)/shard_map/ypk,kn->ypn/dot_general | solution.py:53
  300.1 6.4 %reshape.207 = bf16[1,24,98304]{2,1,0:T(8,128)(2,1)} reshape(bf16[24,768,128]{2,1,0:T(8,128)(2,1)} %fusion.6) | data formatting | bytes 9437184 | tf_op jit(solution)/shard_map/reshape | solution.py:159
  (80 shorter events, 2.6 us)
Async XLA Ops:
  6.5 128.3 %copy-start = (f32[128,1536]{1,0:T(8,128)S(1)}, f32[128,1536]{1,0:T(8,128)}, u32[]{:S(2)}) copy-start(f32[128,1536]{1,0:T(8,128)} %param.16) | copy-start | bytes 2359300
  6.5 70.9 %copy-start.20 = (s32[8,2]{0,1:T(2,128)S(1)}, s32[8,2]{0,1:T(2,128)}, u32[]{:S(2)}) copy-start(s32[8,2]{0,1:T(2,128)} %param.13) | copy-start | bytes 196
  6.5 72.3 %copy-start.7 = (s32[1,48,192]{2,1,0:T(8,128)S(1)}, s32[1,48,192]{2,1,0:T(8,128)}, u32[]{:S(2)}) copy-start(s32[1,48,192]{2,1,0:T(8,128)} %param.14) | copy-start | bytes 110596
  6.5 73.5 %copy-start.12 = (bf16[3,3,64,64]{3,2,1,0:T(8,128)(2,1)S(1)}, bf16[3,3,64,64]{3,2,1,0:T(8,128)(2,1)}, u32[]{:S(2)}) copy-start(bf16[3,3,64,64]{3,2,1,0:T(8,128)(2,1)} %param.18) | copy-start | bytes 221188
  6.5 73.9 %copy-start.15 = (f32[16,64]{1,0:T(8,128)S(1)}, f32[16,64]{1,0:T(8,128)}, u32[]{:S(2)}) copy-start(f32[16,64]{1,0:T(8,128)} %param.20) | copy-start | bytes 12292
  6.5 62.8 %all-gather.2.cloned.1.call-start = ((), (), s32[]{:S(2)}) async-start(), calls=%async_computation.2 | async-start | bytes 6127616 | tf_op jit(solution)/shard_map/all_gather | solution.py:76
  7.3 106.1 %reduce-scatter.2.cloned.1.call-start = ((), (), s32[]{:S(2)}) async-start(), calls=%async_computation.3 | async-start | bytes 3538944 | tf_op jit(solution)/shard_map/reduce_scatter | solution.py:97
  72.8 10.5 %copy-start.16 = (f32[16,64]{1,0:T(8,128)S(1)}, f32[16,64]{1,0:T(8,128)}, u32[]{:S(2)}) copy-start(f32[16,64]{1,0:T(8,128)} %param.21) | copy-start | bytes 12292
  77.4 8.8 %copy-start.13 = (bf16[3,3,64,64]{3,2,1,0:T(8,128)(2,1)S(1)}, bf16[3,3,64,64]{3,2,1,0:T(8,128)(2,1)}, u32[]{:S(2)}) copy-start(bf16[3,3,64,64]{3,2,1,0:T(8,128)(2,1)} %param.19) | copy-start | bytes 221188
  80.4 42.0 %copy-start.18 = (bf16[3,384,128]{2,1,0:T(8,128)(2,1)}, bf16[3,384,128]{2,1,0:T(8,128)(2,1)S(1)}, u32[]{:S(2)}) copy-start(bf16[3,384,128]{2,1,0:T(8,128)(2,1)S(1)} %constant_dynamic-update-slice_fusion) | copy-start | bytes 884740
  115.2 16.4 %all-to-all-start = ((f32[1,384,1,256]{3,0,2,1:T(1,128)}), f32[1,384,1,256]{3,0,2,1:T(1,128)S(1)}, u32[]{:S(2)}, u32[]{:S(2)}) async-start(f32[1,384,1,256]{3,0,2,1:T(1,128)} %copy.41), calls=%async_computation.1 | async-start | bytes 786432 | tf_op jit(solution)/shard_map/all_to_all | solution.py:109
  131.6 9.0 %copy-start.14 = (f32[32,64]{1,0:T(8,128)S(1)}, f32[32,64]{1,0:T(8,128)}, u32[]{:S(2)}) copy-start(f32[32,64]{1,0:T(8,128)} %param.17) | copy-start | bytes 24580
  172.5 12.7 %copy-start.11 = (pred[768,128]{1,0:T(8,128)(4,1)S(1)}, pred[768,128]{1,0:T(8,128)(4,1)}, u32[]{:S(2)}) copy-start(pred[768,128]{1,0:T(8,128)(4,1)} %add_compare_fusion) | copy-start | bytes 294916
  172.5 12.7 %copy-start.21 = (pred[24]{0:T(512)(128)(4,1)S(1)}, pred[24]{0:T(512)(128)(4,1)}, u32[]{:S(2)}) copy-start(pred[24]{0:T(512)(128)(4,1)} %compare_and_fusion) | copy-start | bytes 76
  172.5 23.5 %copy-start.9 = (bf16[3,64,64]{2,1,0:T(8,128)(2,1)S(1)}, bf16[3,64,64]{2,1,0:T(8,128)(2,1)}, u32[]{:S(2)}) copy-start(bf16[3,64,64]{2,1,0:T(8,128)(2,1)} %get-tuple-element.21) | copy-start | bytes 73732
  172.5 23.6 %copy-start.10 = (bf16[3,64,64]{2,1,0:T(8,128)(2,1)S(1)}, bf16[3,64,64]{2,1,0:T(8,128)(2,1)}, u32[]{:S(2)}) copy-start(bf16[3,64,64]{2,1,0:T(8,128)(2,1)} %get-tuple-element.20) | copy-start | bytes 73732
  172.5 24.3 %copy-start.8 = (bf16[3,64,64]{2,1,0:T(8,128)(2,1)S(1)}, bf16[3,64,64]{2,1,0:T(8,128)(2,1)}, u32[]{:S(2)}) copy-start(bf16[3,64,64]{2,1,0:T(8,128)(2,1)} %get-tuple-element.19) | copy-start | bytes 73732
  190.1 26.4 %copy-start.2 = (bf16[24,768,128]{2,1,0:T(8,128)(2,1)}, bf16[24,768,128]{2,1,0:T(8,128)(2,1)S(1)}, u32[]{:S(2)}) copy-start(bf16[24,768,128]{2,1,0:T(8,128)(2,1)S(1)} %fusion.3) | copy-start | bytes 14155780
  190.2 7.6 %collective-permute-start = (bf16[1,768,128]{2,1,0:T(8,128)(2,1)S(1)}, bf16[1,768,128]{2,1,0:T(8,128)(2,1)S(1)}, u32[]{:S(2)}, u32[]{:S(2)}) collective-permute-start(bf16[1,768,128]{2,1,0:T(8,128)(2,1)S(1)} %get-tuple-element.11), channel_id=1, source_target_pairs={{0,1},{1,2},{2,3},{3,4},{4,5},{5,6},{6,7},{7,8},{8,9},{9,10},{10,1... | collective-permute-start | bytes 589832 | tf_op jit(solution)/shard_map/ppermute | solution.py:15
  193.6 9.7 %collective-permute-start.1 = (bf16[1,768,128]{2,1,0:T(8,128)(2,1)S(1)}, bf16[1,768,128]{2,1,0:T(8,128)(2,1)S(1)}, u32[]{:S(2)}, u32[]{:S(2)}) collective-permute-start(bf16[1,768,128]{2,1,0:T(8,128)(2,1)S(1)} %get-tuple-element.12), channel_id=1, source_target_pairs={{1,0},{2,1},{3,2},{4,3},{5,4},{6,5},{7,6},{8,7},{9,8},{10,9},{11,1... | collective-permute-start | bytes 589832 | tf_op jit(solution)/shard_map/ppermute | solution.py:17
  203.9 4.1 %copy-start.19 = (bf16[3,384,128]{2,1,0:T(8,128)(2,1)S(1)}, bf16[3,384,128]{2,1,0:T(8,128)(2,1)}, u32[]{:S(2)}) copy-start(bf16[3,384,128]{2,1,0:T(8,128)(2,1)} %copy-done.18) | copy-start | bytes 884740
  208.0 8.6 %copy-start.3 = (bf16[26,768,128]{2,1,0:T(8,128)(2,1)}, bf16[26,768,128]{2,1,0:T(8,128)(2,1)S(1)}, u32[]{:S(2)}) copy-start(bf16[26,768,128]{2,1,0:T(8,128)(2,1)S(1)} %get-tuple-element.7) | copy-start | bytes 15335428
  208.0 8.6 %copy-start.4 = (bf16[26,768,128]{2,1,0:T(8,128)(2,1)}, bf16[26,768,128]{2,1,0:T(8,128)(2,1)S(1)}, u32[]{:S(2)}) copy-start(bf16[26,768,128]{2,1,0:T(8,128)(2,1)S(1)} %get-tuple-element.8) | copy-start | bytes 15335428
  236.2 24.2 %copy-start.17 = (bf16[3,384,128]{2,1,0:T(8,128)(2,1)S(1)}, bf16[3,384,128]{2,1,0:T(8,128)(2,1)}, u32[]{:S(2)}) copy-start(bf16[3,384,128]{2,1,0:T(8,128)(2,1)} %maximum_dynamic-update-slice_fusion.2) | copy-start | bytes 884740
  254.5 7.6 %collective-permute-start.2 = (bf16[1,768,128]{2,1,0:T(8,128)(2,1)S(1)}, bf16[1,768,128]{2,1,0:T(8,128)(2,1)S(1)}, u32[]{:S(2)}, u32[]{:S(2)}) collective-permute-start(bf16[1,768,128]{2,1,0:T(8,128)(2,1)S(1)} %get-tuple-element.9), channel_id=1, source_target_pairs={{0,1},{1,2},{2,3},{3,4},{4,5},{5,6},{6,7},{7,8},{8,9},{9,10},{10,1... | collective-permute-start | bytes 589832 | tf_op jit(solution)/shard_map/ppermute | solution.py:15
  256.5 9.7 %collective-permute-start.3 = (bf16[1,768,128]{2,1,0:T(8,128)(2,1)S(1)}, bf16[1,768,128]{2,1,0:T(8,128)(2,1)S(1)}, u32[]{:S(2)}, u32[]{:S(2)}) collective-permute-start(bf16[1,768,128]{2,1,0:T(8,128)(2,1)S(1)} %get-tuple-element.10), channel_id=1, source_target_pairs={{1,0},{2,1},{3,2},{4,3},{5,4},{6,5},{7,6},{8,7},{9,8},{10,9},{11,1... | collective-permute-start | bytes 589832 | tf_op jit(solution)/shard_map/ppermute | solution.py:17
  270.9 8.1 %copy-start.5 = (bf16[26,768,128]{2,1,0:T(8,128)(2,1)}, bf16[26,768,128]{2,1,0:T(8,128)(2,1)S(1)}, u32[]{:S(2)}) copy-start(bf16[26,768,128]{2,1,0:T(8,128)(2,1)S(1)} %get-tuple-element.5) | copy-start | bytes 15335428
  270.9 8.1 %copy-start.6 = (bf16[26,768,128]{2,1,0:T(8,128)(2,1)}, bf16[26,768,128]{2,1,0:T(8,128)(2,1)S(1)}, u32[]{:S(2)}) copy-start(bf16[26,768,128]{2,1,0:T(8,128)(2,1)S(1)} %get-tuple-element.6) | copy-start | bytes 15335428
  270.9 15.4 %slice-start = ((s8[4718592]{0:T(1024)(128)(4,1)}), s8[4194304]{0:T(1024)(128)(4,1)S(1)}, s32[]{:S(2)}) async-start(s8[4718592]{0:T(1024)(128)(4,1)} %bitcast.99), calls=%async_computation.4 | async-start | bytes 8388608
  278.9 7.4 %slice-start.1 = ((s8[4718592]{0:T(1024)(128)(4,1)}), s8[524288]{0:T(1024)(128)(4,1)S(1)}, s32[]{:S(2)}) async-start(s8[4718592]{0:T(1024)(128)(4,1)} %bitcast.99), calls=%async_computation.5 | async-start | bytes 1048576
  286.3 20.3 %copy-start.1 = (f32[128,1536]{1,0:T(8,128)S(1)}, f32[128,1536]{1,0:T(8,128)}, u32[]{:S(2)}) copy-start(f32[128,1536]{1,0:T(8,128)} %param.16) | copy-start | bytes 2359300
Sparse Core Ops, SparseCore 0:
  9.5 59.7 all-gather.1
  77.5 35.7 reduce-scatter.1
where the time goes:
time: 314 us; the launch traced here: 313 us
  matrix products  107 us (34%)
  waiting for transfers between devices  98 us (31%)
  local copies, waits for them, and re-layouts  60.8 us (19%)
  starting transfers between devices  18.9 us (6%)
  between operations  15.2 us (5%)
  other arithmetic  13.4 us (4%)
    dot_general x6, matrix products, conv_pairs(): jnp.einsum('ypk,kn->ypn', stacked[shift_row:shift_row + out_rows], weight...  63.4 us
    all_gather x1, waiting for transfers between devices, local(): band = lax.all_gather(coarse, 'slab', axis=1, tiled=True)  59.4 us
    dot_general x1, matrix products, local(): jnp.einsum('ycx,cd->yxd', upsampled, lift, precision=lax.Precision.HIGHEST)  31.9 us
    reduce_scatter x1, waiting for transfers between devices, local(): lax.psum_scatter(jnp.einsum('ykb,rkjbw->ryjw', rows_full, blocks, precisi...  26.5 us
    reshape x1, local copies, waits for them, and re-layouts, local(): lifted = lifted.reshape(rows_dev, pair_count, 2 * channels)  12.7 us
    ppermute x2, waiting for transfers between devices, extended(): lax.ppermute(head, axis, [((i + 1) % count, i) for i in range(ends)])  9.52 us
    slice x2, local copies, waits for them, and re-layouts, conv_pairs(): widened[:, 0:pair_count]  8.07 us
    all_to_all x1, starting transfers between devices, local(): lax.all_to_all(partial_cols, 'slab', split_axis=1, concat_axis=2, tiled=T...  7.14 us
  transfers between devices with their start and end apart: 7, of which 6 were waited for; matrix products, arithmetic and copies ran while one was open for 7% of the time, Pallas kernels for 0%

commit v1 on v0

--- a/solution.py
+++ b/solution.py
@@ -2,6 +2,11 @@
 import jax.numpy as jnp
 from jax import lax
 from jax.sharding import PartitionSpec as P
+
+
+def group_roots(body, along_axis):
+    carry_in = jnp.stack([body for _ in range(jax.lax.psum(1, along_axis))])
+    return jnp.concatenate(jax.lax.all_to_all(carry_in, along_axis, 0, 0), axis=1)
 
 
 def extended(cells, sides, width):
@@ -73,7 +78,7 @@
     gain_table,
     shift_table,
 ):
-    band = lax.all_gather(coarse, "slab", axis=1, tiled=True)
+    band = group_roots(coarse, "slab")
     n_slab = lax.axis_size("slab")
     owner = lax.axis_index("region")
     slab_index = lax.axis_index("slab")

time: 314 us -> 372 us (1.18); the launches traced: 313 us -> 366 us
  waiting for transfers between devices: 98 us -> 134 us
  local copies, waits for them, and re-layouts: 60.8 us -> 68.8 us
  starting transfers between devices: 18.9 us -> 26.2 us
    all_to_all x0 -> x1, waiting for transfers between devices: none -> 79.3 us  [group_roots(): jax.lax.all_to_all(carry_in, along_axis, 0, 0)]
    all_gather x1 -> x0, waiting for transfers between devices: 59.4 us -> none  [local(): band = lax.all_gather(coarse, 'slab', axis=1, tiled=True)]
    reduce_scatter x1, waiting for transfers between devices: 26.5 us -> 43.6 us  [local(): lax.psum_scatter(jnp.einsum('ykb,rkjbw->ryjw', rows_full, blocks, precisi...]
    all_to_all x0 -> x1, starting transfers between devices: none -> 6.99 us  [group_roots(): jax.lax.all_to_all(carry_in, along_axis, 0, 0)]
    all_to_all x0 -> x1, local copies, waits for them, and re-layouts: none -> 5.65 us  [group_roots(): jax.lax.all_to_all(carry_in, along_axis, 0, 0)]
    another operation x0 -> x1, local copies, waits for them, and re-layouts: none -> 4.15 us  [group_roots(): carry_in = jnp.stack([body for _ in range(jax.lax.psum(1, along_axis))])]
  transfers between devices with their start and end apart: 7 -> 7, of which waited for: 6 -> 6; matrix products, arithmetic and copies ran while one was open for 7% -> 5% of each run, Pallas kernels for 0% -> 0%
where the time goes in v1:
time: 372 us; the launch traced here: 366 us
  waiting for transfers between devices  134 us (36%)
  matrix products  108 us (29%)
  local copies, waits for them, and re-layouts  68.8 us (18%)
  starting transfers between devices  26.2 us (7%)
  between operations  15.4 us (4%)
  other arithmetic  13.7 us (4%)
    all_to_all x1, waiting for transfers between devices, group_roots(): jax.lax.all_to_all(carry_in, along_axis, 0, 0)  79.3 us
    dot_general x6, matrix products, conv_pairs(): jnp.einsum('ypk,kn->ypn', stacked[shift_row:shift_row + out_rows], weight...  63.6 us
    reduce_scatter x1, waiting for transfers between devices, local(): lax.psum_scatter(jnp.einsum('ykb,rkjbw->ryjw', rows_full, blocks, precisi...  43.6 us
    dot_general x1, matrix products, local(): jnp.einsum('ycx,cd->yxd', upsampled, lift, precision=lax.Precision.HIGHEST)  32.2 us
    reshape x1, local copies, waits for them, and re-layouts, local(): lifted = lifted.reshape(rows_dev, pair_count, 2 * channels)  12.7 us
    ppermute x2, waiting for transfers between devices, extended(): lax.ppermute(head, axis, [((i + 1) % count, i) for i in range(ends)])  9.53 us
    slice x2, local copies, waits for them, and re-layouts, conv_pairs(): widened[:, 0:pair_count]  8.07 us
    all_to_all x1, starting transfers between devices, local(): lax.all_to_all(partial_cols, 'slab', split_axis=1, concat_axis=2, tiled=T...  7.5 us
  transfers between devices with their start and end apart: 7, of which 6 were waited for; matrix products, arithmetic and copies ran while one was open for 5% of the time, Pallas kernels for 0%

profile of v1, /device:TPU:96, one launch (start us, length us, event | category | flops | bytes accessed | tf_op | source)
XLA Modules:
  0.0 366.1 jit_solution(14886868510685612593)
XLA Ops:
  6.5 4.2 %stack.2 = f32[16,4,11,8,256]{4,3,2,1,0:T(8,128)} broadcast(f32[4,11,8,256]{3,2,1,0:T(8,128)} %param.11), dimensions={1,2,3,4} | broadcast | bytes 6127616 | tf_op jit(solution)/shard_map/stack | solution.py:8
  10.7 7.0 %all-to-all-start = ((f32[16,4,11,8,256]{4,3,2,1,0:T(8,128)}), f32[16,4,11,8,256]{4,3,2,1,0:T(8,128)}, u32[]{:S(2)}, u32[]{:S(2)}) async-start(f32[16,4,11,8,256]{4,3,2,1,0:T(8,128)} %stack.2), calls=%async_computation | async-start | bytes 11534336 | tf_op jit(solution)/shard_map/all_to_all | solution.py:9
  18.5 79.3 %all-to-all-done = f32[16,4,11,8,256]{4,3,2,1,0:T(8,128)} async-done(((f32[16,4,11,8,256]{4,3,2,1,0:T(8,128)}), f32[16,4,11,8,256]{4,3,2,1,0:T(8,128)}, u32[]{:S(2)}, u32[]{:S(2)}) %all-to-all-start) | async-done | bytes 5767200 | tf_op jit(solution)/shard_map/all_to_all | solution.py:9
  97.8 5.7 %copy.37 = f32[16,4,11,8,256]{4,3,2,0,1:T(8,128)} copy(f32[16,4,11,8,256]{4,3,2,1,0:T(8,128)} %all-to-all-done) | data formatting | bytes 11534336 | tf_op jit(solution)/shard_map/all_to_all | solution.py:9
  103.5 3.5 gather_fusion
  107.0 4.5 %convolution_bitcast_fusion = f32[8,384,1,256]{1,3,0,2:T(8,128)} fusion(f32[8,16,8,256]{3,2,1,0:T(8,128)S(1)} %bitcast.109, pred[8,16]{1,0:T(8,128)(4,1)S(1)} %compare_bitcast_fusion, f32[384,128]{0,1:T(8,128)S(1)} %copy.38), kind=kOutput, calls=%fused_computation.27 | convolution fusion | flops 1208221696 | bytes 4391040 | tf_op jit(solution)/shard_map/ykb,rkjbw->ryjw/dot_general | solution.py:103
  112.9 0.6 gather_fusion.1
  113.5 0.6 constant_dynamic-update-slice_fusion.3
  114.5 0.8 fusion.15
  115.3 2.0 pad_maximum_fusion.4
  117.4 0.8 fusion.14
  118.2 2.0 pad_maximum_fusion.5
  120.2 0.7 slice_bitcast_fusion.12
  120.9 43.6 %reduce-scatter.2.cloned.1.call-done = f32[1,384,1,256]{1,3,0,2:T(8,128)} async-done(((f32[8,384,1,256]{1,3,0,2:T(8,128)}), f32[1,384,1,256]{1,3,0,2:T(8,128)}) %reduce-scatter.2.cloned.1.call-update) | async-done | bytes 393232 | tf_op jit(solution)/shard_map/reduce_scatter | solution.py:102
  164.5 1.9 copy.39
  166.4 7.5 %all-to-all-start.1 = ((f32[1,384,1,256]{3,0,2,1:T(1,128)}), f32[1,384,1,256]{3,0,2,1:T(1,128)S(1)}, u32[]{:S(2)}, u32[]{:S(2)}) async-start(f32[1,384,1,256]{3,0,2,1:T(1,128)} %copy.39), calls=%async_computation.2 | async-start | bytes 786432 | tf_op jit(solution)/shard_map/all_to_all | solution.py:114
  174.4 2.4 copy.44
  176.8 3.4 copy.45
  180.8 1.4 pad_dynamic-update-slice_fusion.1
  182.3 0.8 add_compare_fusion
  183.1 0.8 copy.52
  183.9 2.5 reshape_squeeze.3
  186.4 5.7 %fusion.10 = f32[24,32,1536,1]{2,1,0,3:T(8,128)S(1)} fusion(f32[24,16,8,32]{3,2,0,1:T(8,128)} %reshape_squeeze.3, f32[128,1536]{1,0:T(8,128)S(1)} %copy-done), kind=kOutput, calls=%fused_computation.29 | convolution fusion | flops 1811939328 | bytes 5898240 | tf_op jit(solution)/shard_map/ykwc,kwx->ycx/dot_general | solution.py:119
  192.1 32.2 %fusion.7 = bf16[24,1536,64]{2,1,0:T(8,128)(2,1)} fusion(f32[24,32,1536,1]{2,1,0,3:T(8,128)S(1)} %fusion.10, f32[32,64]{1,0:T(8,128)S(1)} %copy-done.16), kind=kOutput, calls=%fused_computation.23 | convolution fusion | flops 905969664 | bytes 9445376 | tf_op jit(solution)/shard_map/ycx,cd->yxd/dot_general | solution.py:120
  224.3 12.7 %reshape.216 = bf16[24,768,128]{2,1,0:T(8,128)(2,1)} reshape(bf16[24,1536,64]{2,1,0:T(8,128)(2,1)} %fusion.7) | data formatting | bytes 9437184 | tf_op jit(solution)/shard_map/reshape | solution.py:121
  237.1 4.9 %fusion.3 = bf16[24,768,128]{2,1,0:T(8,128)(2,1)S(1)} fusion(bf16[24,768,128]{2,1,0:T(8,128)(2,1)} %reshape.216, pred[768,128]{1,0:T(8,128)(4,1)S(1)} %copy-done.11, pred[24]{0:T(512)(128)(4,1)S(1)} %copy-done.23), kind=kLoop, calls=%fused_computation.13 | loop fusion | flops 18874368 | bytes 9535512 | tf_op jit(solution)/shard_map/convert_element_type | solution.py:138
  242.0 3.4 collective-permute-start
  245.4 2.5 collective-permute-start.1
  247.9 0.7 maximum_dynamic-update-slice_fusion.3
  248.6 0.7 maximum_dynamic-update-slice_fusion.2
  249.6 5.5 %collective-permute-done.1 = bf16[1,768,128]{2,1,0:T(8,128)(2,1)S(1)} collective-permute-done((bf16[1,768,128]{2,1,0:T(8,128)(2,1)S(1)}, bf16[1,768,128]{2,1,0:T(8,128)(2,1)S(1)}, u32[]{:S(2)}, u32[]{:S(2)}) %collective-permute-start.1) | collective-permute-done | bytes 196640 | tf_op jit(solution)/shard_map/ppermute | solution.py:22
  255.1 0.8 pad_maximum_fusion.2
  255.9 4.0 %pad_slice_fusion.3 = (bf16[26,768,128]{2,1,0:T(8,128)(2,1)S(1)}, bf16[26,768,128]{2,1,0:T(8,128)(2,1)S(1)}) fusion(bf16[26,768,128]{2,1,0:T(8,128)(2,1)S(1)} %pad_maximum_fusion.2), kind=kLoop, calls=%fused_computation.20 | loop fusion | bytes 15335424 | tf_op jit(solution)/shard_map/slice | solution.py:53
  260.0 8.6 %fusion.21 = f32[24,768,128]{2,1,0:T(8,128)} fusion(bf16[3,384,128]{2,1,0:T(8,128)(2,1)S(1)} %copy-done.21, bf16[26,768,128]{2,1,0:T(8,128)(2,1)S(1)} %get-tuple-element.8, bf16[1,768,128]{2,1,0:T(8,128)(2,1)S(1)} %collective-permute-done.1, bf16[24,768,128]{2,1,0:T(8,128)(2,1)S(1)} %fusion.3, bf16[1,768,128]{2,1,0:T(8,128)(2,1)S(1)} %collective-permute-done, ...), kind=kOutput, calls=%fused_computation.47 | convolution fusion | flops 1888616448 | bytes 24870912 | tf_op jit(solution)/shard_map/ypk,kn->ypn/dot_general | solution.py:58
  268.7 7.3 %fusion.22 = f32[24,768,128]{2,1,0:T(8,128)} fusion(bf16[3,384,128]{2,1,0:T(8,128)(2,1)S(1)} %copy-done.21, bf16[26,768,128]{2,1,0:T(8,128)(2,1)S(1)} %get-tuple-element.8, bf16[1,768,128]{2,1,0:T(8,128)(2,1)S(1)} %collective-permute-done.1, bf16[24,768,128]{2,1,0:T(8,128)(2,1)S(1)} %fusion.3, bf16[1,768,128]{2,1,0:T(8,128)(2,1)S(1)} %collective-permute-done, ...), kind=kOutput, calls=%fused_computation.49 | convolution fusion | flops 1888616448 | bytes 24870912 | tf_op jit(solution)/shard_map/ypk,kn->ypn/dot_general | solution.py:58
  276.0 5.3 %mul.53 = f32[24,192,4,128]{3,2,1,0:T(4,128)} broadcast(f32[24,192,128]{2,1,0:T(8,128)S(1)} %copy.44), dimensions={0,1,3} | broadcast | bytes 11796480 | tf_op jit(solution)/shard_map/mul | solution.py:157
  281.3 7.0 %add.156 = f32[24,192,4,128]{3,2,1,0:T(4,128)} broadcast(f32[24,192,128]{2,1,0:T(8,128)} %copy.45), dimensions={0,1,3} | broadcast | bytes 11796480 | tf_op jit(solution)/shard_map/add | solution.py:157
  288.3 18.3 %fusion.5 = bf16[24,768,128]{2,1,0:T(8,128)(2,1)S(1)} fusion(f32[24,768,128]{2,1,0:T(8,128)} %bitcast.106, f32[24,768,128]{2,1,0:T(8,128)} %bitcast.105, f32[24,768,128]{2,1,0:T(8,128)} %fusion.22, f32[24,768,128]{2,1,0:T(8,128)} %fusion.21, pred[768,128]{1,0:T(8,128)(4,1)S(1)} %copy-done.11, pred[24]{0:T(512)(128)(4,1)S(1)} %copy-done.23, ...), kind=kOutput, calls=%fused_computation.15 | convolution fusion | flops 1914568704 | bytes 57999872 | tf_op jit(solution)/shard_map/ypk,kn->ypn/dot_general | solution.py:58
  306.7 1.9 collective-permute-start.2
  308.6 3.9 %collective-permute-start.3 = (bf16[1,768,128]{2,1,0:T(8,128)(2,1)S(1)}, bf16[1,768,128]{2,1,0:T(8,128)(2,1)S(1)}, u32[]{:S(2)}, u32[]{:S(2)}) collective-permute-start(bf16[1,768,128]{2,1,0:T(8,128)(2,1)S(1)} %get-tuple-element.10), channel_id=1, source_target_pairs={{1,0},{2,1},{3,2},{4,3},{5,4},{6,5},{7,6},{8,7},{9,8},{10,9},{11,1... | collective-permute-start | bytes 589832 | tf_op jit(solution)/shard_map/ppermute | solution.py:22
  312.6 1.6 collective-permute-done.2
  314.2 4.0 %collective-permute-done.3 = bf16[1,768,128]{2,1,0:T(8,128)(2,1)S(1)} collective-permute-done((bf16[1,768,128]{2,1,0:T(8,128)(2,1)S(1)}, bf16[1,768,128]{2,1,0:T(8,128)(2,1)S(1)}, u32[]{:S(2)}, u32[]{:S(2)}) %collective-permute-start.3) | collective-permute-done | bytes 196640 | tf_op jit(solution)/shard_map/ppermute | solution.py:22
  318.3 0.9 pad_maximum_fusion.3
  319.2 4.0 %pad_slice_fusion.1 = (bf16[26,768,128]{2,1,0:T(8,128)(2,1)S(1)}, bf16[26,768,128]{2,1,0:T(8,128)(2,1)S(1)}) fusion(bf16[26,768,128]{2,1,0:T(8,128)(2,1)S(1)} %pad_maximum_fusion.3), kind=kLoop, calls=%fused_computation.18 | loop fusion | bytes 15335424 | tf_op jit(solution)/shard_map/slice | solution.py:53
  323.2 8.1 %fusion.19 = f32[24,768,128]{2,1,0:T(8,128)} fusion(bf16[3,384,128]{2,1,0:T(8,128)(2,1)S(1)} %constant_dynamic-update-slice_fusion.2, bf16[26,768,128]{2,1,0:T(8,128)(2,1)S(1)} %get-tuple-element.6, bf16[1,768,128]{2,1,0:T(8,128)(2,1)S(1)} %collective-permute-done.3, bf16[24,768,128]{2,1,0:T(8,128)(2,1)S(1)} %fusion.5, ...), kind=kOutput, calls=%fused_computation.42 | convolution fusion | flops 1888616448 | bytes 24870912 | tf_op jit(solution)/shard_map/ypk,kn->ypn/dot_general | solution.py:58
  331.3 7.4 %fusion.20 = f32[24,768,128]{2,1,0:T(8,128)} fusion(bf16[3,384,128]{2,1,0:T(8,128)(2,1)S(1)} %constant_dynamic-update-slice_fusion.2, bf16[26,768,128]{2,1,0:T(8,128)(2,1)S(1)} %get-tuple-element.6, bf16[1,768,128]{2,1,0:T(8,128)(2,1)S(1)} %collective-permute-done.3, bf16[24,768,128]{2,1,0:T(8,128)(2,1)S(1)} %fusion.5, ...), kind=kOutput, calls=%fused_computation.44 | convolution fusion | flops 1888616448 | bytes 24870912 | tf_op jit(solution)/shard_map/ypk,kn->ypn/dot_general | solution.py:58
  338.7 13.8 %fusion.6 = bf16[24,768,128]{2,1,0:T(8,128)(2,1)} fusion(f32[24,768,128]{2,1,0:T(8,128)} %fusion.20, f32[24,768,128]{2,1,0:T(8,128)} %fusion.19, pred[768,128]{1,0:T(8,128)(4,1)S(1)} %copy-done.11, pred[24]{0:T(512)(128)(4,1)S(1)} %copy-done.23, bf16[3,384,128]{2,1,0:T(8,128)(2,1)S(1)} %constant_dynamic-update-slice_fusion.2, ...), kind=kOutput, calls=%fused_computation.16 | convolution fusion | flops 1907490816 | bytes 43844096 | tf_op jit(solution)/shard_map/ypk,kn->ypn/dot_general | solution.py:58
  352.6 6.4 %reshape.217 = bf16[1,24,98304]{2,1,0:T(8,128)(2,1)} reshape(bf16[24,768,128]{2,1,0:T(8,128)(2,1)} %fusion.6) | data formatting | bytes 9437184 | tf_op jit(solution)/shard_map/reshape | solution.py:164
  (85 shorter events, 2.9 us)
Async XLA Ops:
  6.5 179.8 %copy-start = (f32[128,1536]{1,0:T(8,128)S(1)}, f32[128,1536]{1,0:T(8,128)}, u32[]{:S(2)}) copy-start(f32[128,1536]{1,0:T(8,128)} %param.16) | copy-start | bytes 2359300
  6.5 11.2 %copy-start.12 = (s32[8,16,16,3]{2,1,3,0:T(8,128)S(1)}, s32[8,16,16,3]{2,1,3,0:T(8,128)}, u32[]{:S(2)}) copy-start(s32[8,16,16,3]{2,1,3,0:T(8,128)} %param.12) | copy-start | bytes 73732
  6.5 11.8 %copy-start.13 = (f32[384,128]{1,0:T(8,128)S(1)}, f32[384,128]{1,0:T(8,128)}, u32[]{:S(2)}) copy-start(f32[384,128]{1,0:T(8,128)} %param.15) | copy-start | bytes 589828
  10.7 87.1 %all-to-all-start = ((f32[16,4,11,8,256]{4,3,2,1,0:T(8,128)}), f32[16,4,11,8,256]{4,3,2,1,0:T(8,128)}, u32[]{:S(2)}, u32[]{:S(2)}) async-start(f32[16,4,11,8,256]{4,3,2,1,0:T(8,128)} %stack.2), calls=%async_computation | async-start | bytes 11534336 | tf_op jit(solution)/shard_map/all_to_all | solution.py:9
  17.7 146.8 %reduce-scatter.2.cloned.1.call-start = ((), (), s32[]{:S(2)}) async-start(), calls=%async_computation.3 | async-start | bytes 3538944 | tf_op jit(solution)/shard_map/reduce_scatter | solution.py:102
  107.0 4.6 %copy-start.22 = (s32[8,2]{0,1:T(2,128)S(1)}, s32[8,2]{0,1:T(2,128)}, u32[]{:S(2)}) copy-start(s32[8,2]{0,1:T(2,128)} %param.13) | copy-start | bytes 196
  107.0 5.9 %copy-start.7 = (s32[1,48,192]{2,1,0:T(8,128)S(1)}, s32[1,48,192]{2,1,0:T(8,128)}, u32[]{:S(2)}) copy-start(s32[1,48,192]{2,1,0:T(8,128)} %param.14) | copy-start | bytes 110596
  107.0 7.2 %copy-start.14 = (bf16[3,3,64,64]{3,2,1,0:T(8,128)(2,1)S(1)}, bf16[3,3,64,64]{3,2,1,0:T(8,128)(2,1)}, u32[]{:S(2)}) copy-start(bf16[3,3,64,64]{3,2,1,0:T(8,128)(2,1)} %param.18) | copy-start | bytes 221188
  107.0 7.5 %copy-start.17 = (f32[16,64]{1,0:T(8,128)S(1)}, f32[16,64]{1,0:T(8,128)}, u32[]{:S(2)}) copy-start(f32[16,64]{1,0:T(8,128)} %param.20) | copy-start | bytes 12292
  111.5 5.9 %copy-start.18 = (f32[16,64]{1,0:T(8,128)S(1)}, f32[16,64]{1,0:T(8,128)}, u32[]{:S(2)}) copy-start(f32[16,64]{1,0:T(8,128)} %param.21) | copy-start | bytes 12292
  111.5 8.8 %copy-start.15 = (bf16[3,3,64,64]{3,2,1,0:T(8,128)(2,1)S(1)}, bf16[3,3,64,64]{3,2,1,0:T(8,128)(2,1)}, u32[]{:S(2)}) copy-start(bf16[3,3,64,64]{3,2,1,0:T(8,128)(2,1)} %param.19) | copy-start | bytes 221188
  114.5 59.4 %copy-start.20 = (bf16[3,384,128]{2,1,0:T(8,128)(2,1)}, bf16[3,384,128]{2,1,0:T(8,128)(2,1)S(1)}, u32[]{:S(2)}) copy-start(bf16[3,384,128]{2,1,0:T(8,128)(2,1)S(1)} %constant_dynamic-update-slice_fusion) | copy-start | bytes 884740
  166.4 16.7 %all-to-all-start.1 = ((f32[1,384,1,256]{3,0,2,1:T(1,128)}), f32[1,384,1,256]{3,0,2,1:T(1,128)S(1)}, u32[]{:S(2)}, u32[]{:S(2)}) async-start(f32[1,384,1,256]{3,0,2,1:T(1,128)} %copy.39), calls=%async_computation.2 | async-start | bytes 786432 | tf_op jit(solution)/shard_map/all_to_all | solution.py:114
  183.1 9.0 %copy-start.16 = (f32[32,64]{1,0:T(8,128)S(1)}, f32[32,64]{1,0:T(8,128)}, u32[]{:S(2)}) copy-start(f32[32,64]{1,0:T(8,128)} %param.17) | copy-start | bytes 24580
  224.3 12.7 %copy-start.11 = (pred[768,128]{1,0:T(8,128)(4,1)S(1)}, pred[768,128]{1,0:T(8,128)(4,1)}, u32[]{:S(2)}) copy-start(pred[768,128]{1,0:T(8,128)(4,1)} %add_compare_fusion) | copy-start | bytes 294916
  224.3 12.7 %copy-start.23 = (pred[24]{0:T(512)(128)(4,1)S(1)}, pred[24]{0:T(512)(128)(4,1)}, u32[]{:S(2)}) copy-start(pred[24]{0:T(512)(128)(4,1)} %compare_and_fusion) | copy-start | bytes 76
  224.3 23.5 %copy-start.9 = (bf16[3,64,64]{2,1,0:T(8,128)(2,1)S(1)}, bf16[3,64,64]{2,1,0:T(8,128)(2,1)}, u32[]{:S(2)}) copy-start(bf16[3,64,64]{2,1,0:T(8,128)(2,1)} %get-tuple-element.21) | copy-start | bytes 73732
  224.3 23.6 %copy-start.10 = (bf16[3,64,64]{2,1,0:T(8,128)(2,1)S(1)}, bf16[3,64,64]{2,1,0:T(8,128)(2,1)}, u32[]{:S(2)}) copy-start(bf16[3,64,64]{2,1,0:T(8,128)(2,1)} %get-tuple-element.20) | copy-start | bytes 73732
  224.3 24.3 %copy-start.8 = (bf16[3,64,64]{2,1,0:T(8,128)(2,1)S(1)}, bf16[3,64,64]{2,1,0:T(8,128)(2,1)}, u32[]{:S(2)}) copy-start(bf16[3,64,64]{2,1,0:T(8,128)(2,1)} %get-tuple-element.19) | copy-start | bytes 73732
  242.0 26.7 %copy-start.2 = (bf16[24,768,128]{2,1,0:T(8,128)(2,1)}, bf16[24,768,128]{2,1,0:T(8,128)(2,1)S(1)}, u32[]{:S(2)}) copy-start(bf16[24,768,128]{2,1,0:T(8,128)(2,1)S(1)} %fusion.3) | copy-start | bytes 14155780
  242.0 7.6 %collective-permute-start = (bf16[1,768,128]{2,1,0:T(8,128)(2,1)S(1)}, bf16[1,768,128]{2,1,0:T(8,128)(2,1)S(1)}, u32[]{:S(2)}, u32[]{:S(2)}) collective-permute-start(bf16[1,768,128]{2,1,0:T(8,128)(2,1)S(1)} %get-tuple-element.11), channel_id=1, source_target_pairs={{0,1},{1,2},{2,3},{3,4},{4,5},{5,6},{6,7},{7,8},{8,9},{9,10},{10,1... | collective-permute-start | bytes 589832 | tf_op jit(solution)/shard_map/ppermute | solution.py:20
  245.4 9.7 %collective-permute-start.1 = (bf16[1,768,128]{2,1,0:T(8,128)(2,1)S(1)}, bf16[1,768,128]{2,1,0:T(8,128)(2,1)S(1)}, u32[]{:S(2)}, u32[]{:S(2)}) collective-permute-start(bf16[1,768,128]{2,1,0:T(8,128)(2,1)S(1)} %get-tuple-element.12), channel_id=1, source_target_pairs={{1,0},{2,1},{3,2},{4,3},{5,4},{6,5},{7,6},{8,7},{9,8},{10,9},{11,1... | collective-permute-start | bytes 589832 | tf_op jit(solution)/shard_map/ppermute | solution.py:22
  255.9 4.1 %copy-start.21 = (bf16[3,384,128]{2,1,0:T(8,128)(2,1)S(1)}, bf16[3,384,128]{2,1,0:T(8,128)(2,1)}, u32[]{:S(2)}) copy-start(bf16[3,384,128]{2,1,0:T(8,128)(2,1)} %copy-done.20) | copy-start | bytes 884740
  260.0 8.7 %copy-start.3 = (bf16[26,768,128]{2,1,0:T(8,128)(2,1)}, bf16[26,768,128]{2,1,0:T(8,128)(2,1)S(1)}, u32[]{:S(2)}) copy-start(bf16[26,768,128]{2,1,0:T(8,128)(2,1)S(1)} %get-tuple-element.7) | copy-start | bytes 15335428
  260.0 8.7 %copy-start.4 = (bf16[26,768,128]{2,1,0:T(8,128)(2,1)}, bf16[26,768,128]{2,1,0:T(8,128)(2,1)S(1)}, u32[]{:S(2)}) copy-start(bf16[26,768,128]{2,1,0:T(8,128)(2,1)S(1)} %get-tuple-element.8) | copy-start | bytes 15335428
  288.3 24.2 %copy-start.19 = (bf16[3,384,128]{2,1,0:T(8,128)(2,1)S(1)}, bf16[3,384,128]{2,1,0:T(8,128)(2,1)}, u32[]{:S(2)}) copy-start(bf16[3,384,128]{2,1,0:T(8,128)(2,1)} %maximum_dynamic-update-slice_fusion.2) | copy-start | bytes 884740
  306.7 7.6 %collective-permute-start.2 = (bf16[1,768,128]{2,1,0:T(8,128)(2,1)S(1)}, bf16[1,768,128]{2,1,0:T(8,128)(2,1)S(1)}, u32[]{:S(2)}, u32[]{:S(2)}) collective-permute-start(bf16[1,768,128]{2,1,0:T(8,128)(2,1)S(1)} %get-tuple-element.9), channel_id=1, source_target_pairs={{0,1},{1,2},{2,3},{3,4},{4,5},{5,6},{6,7},{7,8},{8,9},{9,10},{10,1... | collective-permute-start | bytes 589832 | tf_op jit(solution)/shard_map/ppermute | solution.py:20
  308.6 9.7 %collective-permute-start.3 = (bf16[1,768,128]{2,1,0:T(8,128)(2,1)S(1)}, bf16[1,768,128]{2,1,0:T(8,128)(2,1)S(1)}, u32[]{:S(2)}, u32[]{:S(2)}) collective-permute-start(bf16[1,768,128]{2,1,0:T(8,128)(2,1)S(1)} %get-tuple-element.10), channel_id=1, source_target_pairs={{1,0},{2,1},{3,2},{4,3},{5,4},{6,5},{7,6},{8,7},{9,8},{10,9},{11,1... | collective-permute-start | bytes 589832 | tf_op jit(solution)/shard_map/ppermute | solution.py:22
  323.2 8.1 %copy-start.5 = (bf16[26,768,128]{2,1,0:T(8,128)(2,1)}, bf16[26,768,128]{2,1,0:T(8,128)(2,1)S(1)}, u32[]{:S(2)}) copy-start(bf16[26,768,128]{2,1,0:T(8,128)(2,1)S(1)} %get-tuple-element.5) | copy-start | bytes 15335428
  323.2 8.1 %copy-start.6 = (bf16[26,768,128]{2,1,0:T(8,128)(2,1)}, bf16[26,768,128]{2,1,0:T(8,128)(2,1)S(1)}, u32[]{:S(2)}) copy-start(bf16[26,768,128]{2,1,0:T(8,128)(2,1)S(1)} %get-tuple-element.6) | copy-start | bytes 15335428
  323.2 15.5 %slice-start = ((s8[4718592]{0:T(1024)(128)(4,1)}), s8[4194304]{0:T(1024)(128)(4,1)S(1)}, s32[]{:S(2)}) async-start(s8[4718592]{0:T(1024)(128)(4,1)} %bitcast.103), calls=%async_computation.4 | async-start | bytes 8388608
  331.3 7.4 %slice-start.1 = ((s8[4718592]{0:T(1024)(128)(4,1)}), s8[524288]{0:T(1024)(128)(4,1)S(1)}, s32[]{:S(2)}) async-start(s8[4718592]{0:T(1024)(128)(4,1)} %bitcast.103), calls=%async_computation.5 | async-start | bytes 1048576
  338.7 20.2 %copy-start.1 = (f32[128,1536]{1,0:T(8,128)S(1)}, f32[128,1536]{1,0:T(8,128)}, u32[]{:S(2)}) copy-start(f32[128,1536]{1,0:T(8,128)} %param.16) | copy-start | bytes 2359300
Sparse Core Ops, SparseCore 0:
  111.6 52.7 reduce-scatter.1
